TPU v7x, 32 devices: a whole 2x2x4 slice. The times are simulated.
32 devices in a mesh: tm: 4 (over y, core), site: 8 (over z, x).
Axes of the slice: x: 2, y: 2, z: 4, core: 2. Of those that a mesh axis runs over, the one named last changes fastest.
Arguments:
- left_modes: bfloat16 [4, 2, 512, 1536], P('tm', None, None, 'site'), may hold values from -6 to 6
- right_modes: bfloat16 [4, 2, 2048, 1536], P('tm', None, None, 'site'), may hold values from -6 to 6
- momenta: int32 [4, 3], P('tm'), may hold values from -3 to 3
- far_fields: bfloat16 [4, 2, 2048, 2048], P('tm', None, None, 'site'), may hold values from -0.09375 to 0.09375
Outputs:
- meson: bfloat16 [4, 2, 512, 2048], P('tm', None, None, 'site')
- product: bfloat16 [4, 2, 512, 2048], P('tm', None, None, 'site')
All inputs are finite; a program needn't handle non-finite values.
Results may differ from a plain program's by a relative error of at most 0.0058.
Values may be sent and summed in bfloat16 or wider, within the bound.
A program may use at most 64 MiB of HBM per device.

v0:
```python
import math

import jax
import jax.numpy as jnp
from jax import lax
from jax.sharding import PartitionSpec as P

SC = 12
EXTENT = 96
SITE_DEV = 16
DT = 3


def shifted(value, axis, steps):
    count = lax.axis_size(axis)
    pairs = [(source, (source + steps) % count) for source in range(count)]
    return lax.ppermute(value, axis, pairs)


def block_coords(sites):
    coord_x = jnp.zeros_like(sites)
    coord_y = jnp.zeros_like(sites)
    coord_z = jnp.zeros_like(sites)
    for level in range(7):
        coord_x = coord_x + sites // 8**level % 2 * 2**level
        coord_y = coord_y + sites // (2 * 8**level) % 2 * 2**level
        coord_z = coord_z + sites // (4 * 8**level) % 2 * 2**level
    return (coord_x, coord_y, coord_z)


def body(left_modes, right_modes, momenta, far_fields):
    groups = lax.axis_size("site")
    factor = (24.0 * SITE_DEV * groups) ** (-0.5)
    sites = lax.axis_index("site") * SITE_DEV + jnp.arange(SITE_DEV, dtype=jnp.int32)
    momentum = momenta[0]
    coord_x, coord_y, coord_z = block_coords(sites)
    wave = (momentum[0] * coord_x + momentum[1] * coord_y + momentum[2] * coord_z) % EXTENT
    angles = 2.0 * math.pi / EXTENT * wave.astype(jnp.float32)
    cosine = jnp.repeat(jnp.cos(angles), SC)
    sine = jnp.repeat(jnp.sin(angles), SC)
    left_real = left_modes[0, 0].astype(jnp.float32)
    left_imag = left_modes[0, 1].astype(jnp.float32)
    phased_real = (factor * (left_real * cosine + left_imag * sine)).astype(jnp.bfloat16)
    phased_imag = (factor * (left_real * sine - left_imag * cosine)).astype(jnp.bfloat16)
    contract = (((1,), (1,)), ((), ()))
    phased_pair = jnp.stack([phased_real, phased_imag])
    left_whole = lax.all_gather(phased_pair, "site", axis=2, tiled=True)
    right_cols = lax.all_to_all(right_modes[0], "site", split_axis=1, concat_axis=2, tiled=True)
    left_joined = jnp.concatenate([left_whole[0], left_whole[1]], axis=1)
    for_real = jnp.concatenate([right_cols[0], -right_cols[1]], axis=1)
    for_imag = jnp.concatenate([right_cols[1], right_cols[0]], axis=1)
    part_real = lax.dot_general(left_joined, for_real, contract, preferred_element_type=jnp.float32)
    part_imag = lax.dot_general(left_joined, for_imag, contract, preferred_element_type=jnp.float32)
    meson_block = jnp.stack([part_real, part_imag]).astype(jnp.bfloat16)
    later_field = shifted(far_fields[0], "tm", -DT)
    field_real = later_field[0]
    field_imag = later_field[1]
    shard_piece = lax.all_gather(meson_block, "site", axis=2, tiled=True)
    joined = jnp.concatenate([shard_piece[0], shard_piece[1]], axis=1)
    stack_real = jnp.concatenate([field_real, -field_imag], axis=0)
    stack_imag = jnp.concatenate([field_imag, field_real], axis=0)
    gained = jnp.stack(
        [
            jnp.dot(joined, stack_real, preferred_element_type=jnp.float32),
            jnp.dot(joined, stack_imag, preferred_element_type=jnp.float32),
        ]
    )
    product_block = gained.astype(jnp.bfloat16)
    return (meson_block[None], product_block[None])


def solution(mesh):
    return jax.shard_map(
        body,
        mesh=mesh,
        in_specs=(
            P("tm", None, None, "site"),
            P("tm", None, None, "site"),
            P("tm", None),
            P("tm", None, None, "site"),
        ),
        out_specs=(P("tm", None, None, "site"), P("tm", None, None, "site")),
        check_vma=False,
    )
```

profile of v0, /device:TPU:0, one launch (start us, length us, event | category | flops | bytes accessed | tf_op | source)
XLA Modules:
  0.0 208.6 jit_solution(10121614878063238395)
XLA Ops:
  7.2 0.0 copy-start
  7.2 0.0 all-gather.3.cloned.1.call-start
  7.2 1.4 fusion.106
  8.6 2.1 fusion.103
  10.7 0.1 broadcast_in_dim.9
  10.8 0.1 mul.187
  10.9 0.1 broadcast_in_dim.8
  11.0 0.1 mul.184
  11.1 1.2 fusion.36
  12.3 0.8 pad_maximum_fusion.21
  13.1 0.0 all-gather.3.cloned.1.call-update
  13.1 0.0 all-gather.5.cloned.1.call-start
  13.2 0.0 copy-done
  13.2 3.8 %copy.8 = bf16[1,2,2048,192]{3,1,2,0:T(2,128)(2,1)} copy(bf16[1,2,2048,192]{2,3,1,0:T(8,128)(2,1)S(1)} %copy-done) | data formatting | bytes 3145728 | tf_op args[1]
  17.0 93.4 %all_to_all.15 = bf16[2,2048,192]{2,0,1:T(2,128)(2,1)S(1)} all-to-all(bf16[2,2048,192]{2,0,1:T(2,128)(2,1)} %bitcast.41), channel_id=1, replica_groups=mesh['tm'=4,'site'=8] {'site'}, dimensions={1} | all-to-all | bytes 3145728 | tf_op jit(solution)/shard_map/all_to_all | solution.py:48
  110.4 3.7 %copy.12 = bf16[2,8,256,192]{2,1,3,0:T(8,128)(2,1)} copy(bf16[2,8,256,192]{3,0,2,1:T(2,128)(2,1)S(1)} %bitcast.40) | data formatting | bytes 3145728 | tf_op jit(solution)/shard_map/all_to_all | solution.py:48
  114.1 1.5 fusion.105
  115.6 0.2 copy.11
  115.7 0.2 copy.10
  115.9 0.1 bitcast_negate_fusion
  116.0 0.0 all-gather.3.cloned.1.call-done
  116.0 2.1 slice_bitcast_fusion.3
  118.1 1.0 fusion.19
  119.1 1.0 fusion.16
  120.2 0.0 copy-start.1
  120.2 0.7 copy-done.1
  120.9 0.8 pad_maximum_fusion.19
  121.7 0.0 all-gather.5.cloned.1.call-update
  121.7 0.1 collective-permute-start
  121.8 25.7 %collective-permute-done = bf16[2,2048,256]{2,1,0:T(8,128)(2,1)S(1)} collective-permute-done((bf16[2,2048,256]{2,1,0:T(8,128)(2,1)}, bf16[2,2048,256]{2,1,0:T(8,128)(2,1)S(1)}, u32[]{:S(2)}, u32[]{:S(2)}) %collective-permute-start) | collective-permute-done | bytes 2097184 | tf_op jit(solution)/shard_map/ppermute | solution.py:17
  147.5 0.1 fusion.102
  147.5 0.0 copy-start.2
  147.6 0.1 slice_bitcast_fusion.4
  147.7 0.8 copy-done.2
  148.5 0.8 pad_maximum_fusion.18
  149.3 46.3 %all-gather.5.cloned.1.call-done = bf16[2,512,2048]{2,1,0:T(8,128)(2,1)} async-done(((bf16[2,512,256]{2,1,0:T(8,128)(2,1)}), bf16[2,512,2048]{2,1,0:T(8,128)(2,1)}) %all-gather.5.cloned.1.call-update) | async-done | bytes 4194320 | tf_op jit(solution)/shard_map/all_gather | solution.py:58
  195.7 2.7 %slice_bitcast_fusion.1 = (bf16[512,2048]{1,0:T(8,128)(2,1)S(1)}, bf16[512,2048]{1,0:T(8,128)(2,1)S(1)}) fusion(bf16[2,512,2048]{2,1,0:T(8,128)(2,1)} %all-gather.5.cloned.1.call-done), kind=kLoop, calls=%fused_computation.5 | loop fusion | bytes 8388608 | tf_op jit(solution)/shard_map/squeeze | solution.py:59
  198.4 1.3 fusion.31
  199.7 1.3 fusion.28
  200.9 0.8 pad_maximum_fusion.20
  (1 shorter events, 0.0 us)
Async XLA Ops:
  7.2 6.0 %copy-start = (bf16[1,2,2048,192]{2,3,1,0:T(8,128)(2,1)S(1)}, bf16[1,2,2048,192]{2,3,1,0:T(8,128)(2,1)}, u32[]{:S(2)}) copy-start(bf16[1,2,2048,192]{2,3,1,0:T(8,128)(2,1)} %param.5) | copy-start | bytes 4718596
  7.2 108.8 %all-gather.3.cloned.1.call-start = ((), (), s32[]{:S(2)}) async-start(), calls=%async_computation.1 | async-start | bytes 3538944 | tf_op jit(solution)/shard_map/all_gather | solution.py:47
  13.1 182.5 %all-gather.5.cloned.1.call-start = ((), (), s32[]{:S(2)}) async-start(), calls=%async_computation.2 | async-start | bytes 4718592 | tf_op jit(solution)/shard_map/all_gather | solution.py:58
  120.2 0.7 copy-start.1
  121.7 25.7 %collective-permute-start = (bf16[2,2048,256]{2,1,0:T(8,128)(2,1)}, bf16[2,2048,256]{2,1,0:T(8,128)(2,1)S(1)}, u32[]{:S(2)}, u32[]{:S(2)}) collective-permute-start(bf16[2,2048,256]{2,1,0:T(8,128)(2,1)} %bitcast.50), channel_id=1, source_target_pairs={{0,8},{8,16},{16,24},{24,0},{1,9},{9,17},{17,25},{25,1},{2,10},{10... | collective-permute-start | bytes 6291464 | tf_op jit(solution)/shard_map/ppermute | solution.py:17
  147.5 1.0 copy-start.2
Sparse Core Ops, SparseCore 0:
  13.2 97.3 all-gather.2
  121.9 73.7 all-gather.4
where the time goes:
time: 209 us
  blocking collectives  93.4 us (45%)
  waiting for transfers between devices  72 us (34%)
  local copies, waits for them, and re-layouts  17.5 us (8%)
  between operations  14.2 us (7%)
  other arithmetic  6.78 us (3%)
  matrix products  4.58 us (2%)
    all_to_all x1, blocking collectives, body(): lax.all_to_all(right_modes[0], 'site', split_axis=1, concat_axis=2, tiled...  93.4 us
    all_gather x1, waiting for transfers between devices, body(): shard_piece = lax.all_gather(meson_block, 'site', axis=2, tiled=True)  46.3 us
    ppermute x1, waiting for transfers between devices, shifted(): return lax.ppermute(value, axis, pairs)  25.7 us
    unnamed x7, local copies, waits for them, and re-layouts  5.33 us
  transfers between devices with their start and end apart: 3, of which 2 were waited for; matrix products, arithmetic and copies ran while one was open for 5% of the time, Pallas kernels for 0%

commit v1 on v0

v1 whole, which is shorter than its diff:
```python
import functools
import math

import jax
import jax.numpy as jnp
from jax import lax
from jax.experimental import pallas as pl
from jax.experimental.pallas import tpu as pltpu
from jax.sharding import PartitionSpec as P

SC = 12
EXTENT = 96
DT = 3
PAIR = 2
MESH = pl.DeviceIdType.MESH
NT = (((1,), (1,)), ((), ()))


def block_coords(sites):
    coord_x = jnp.zeros_like(sites)
    coord_y = jnp.zeros_like(sites)
    coord_z = jnp.zeros_like(sites)
    for level in range(7):
        coord_x = coord_x + sites // 8**level % 2 * 2**level
        coord_y = coord_y + sites // (2 * 8**level) % 2 * 2**level
        coord_z = coord_z + sites // (4 * 8**level) % 2 * 2**level
    return (coord_x, coord_y, coord_z)


def order(k, z, nz):
    short = jnp.minimum(z, nz - 1 - z)
    lone = nz - 1 - 2 * short
    toward = jnp.where(z < nz - 1 - z, 1, -1)
    rest = k - lone
    far = z + toward * (nz - 1 - short - k)
    near = z + (short - rest // 2) * (1 - 2 * (rest % 2))
    return jnp.where(k == nz - 1, z, jnp.where(k < lone, far, near))


def kernel(
    times,
    groups,
    factor,
    left_ref,
    right_ref,
    wave_ref,
    far_ref,
    meson_ref,
    product_ref,
    phased,
    field,
    x_out,
    x_in,
    z_out,
    z_in,
    gathered,
    total,
    far_send,
    far_recv,
    xo_sem,
    xi_sem,
    zo_sem,
    zi_sem,
    g_recv,
    g_up,
    g_down,
    g_pair,
):
    nz = groups // PAIR
    cols = meson_ref.shape[2]
    tm = lax.axis_index("tm")
    me = lax.axis_index("site")
    z = me // PAIR
    x = me % PAIR
    mate = z * PAIR + (1 - x)
    up = me + PAIR
    down = me - PAIR
    has_up = z < nz - 1
    has_down = z > 0
    target = lax.rem(tm + times - DT % times, times)
    source = lax.rem(tm + DT, times)

    barrier = pltpu.get_barrier_semaphore()
    pl.semaphore_signal(barrier, inc=1, device_id=(target, me), device_id_type=MESH)
    pl.semaphore_signal(barrier, inc=1, device_id=(source, me), device_id_type=MESH)
    pl.semaphore_signal(barrier, inc=1, device_id=(tm, mate), device_id_type=MESH)

    @pl.when(has_up)
    def _():
        pl.semaphore_signal(barrier, inc=1, device_id=(tm, up), device_id_type=MESH)

    @pl.when(has_down)
    def _():
        pl.semaphore_signal(barrier, inc=1, device_id=(tm, down), device_id_type=MESH)

    pl.semaphore_wait(barrier, 3 + has_up.astype(jnp.int32) + has_down.astype(jnp.int32))

    def send(src, dst, send_sem, recv_sem, site):
        return pltpu.make_async_remote_copy(
            src_ref=src,
            dst_ref=dst,
            send_sem=send_sem,
            recv_sem=recv_sem,
            device_id=(tm, site),
            device_id_type=MESH,
        )

    far_copy = pltpu.make_async_remote_copy(
        src_ref=far_ref,
        dst_ref=field,
        send_sem=far_send,
        recv_sem=far_recv,
        device_id=(target, me),
        device_id_type=MESH,
    )
    far_copy.start()

    cosine = wave_ref[0:1, :]
    sine = wave_ref[1:2, :]
    real = left_ref[0].astype(jnp.float32)
    imag = left_ref[1].astype(jnp.float32)
    phased[0] = (factor * (real * cosine + imag * sine)).astype(jnp.bfloat16)
    phased[1] = (factor * (real * sine - imag * cosine)).astype(jnp.bfloat16)

    def partial(site):
        rows = pl.ds(pl.multiple_of(site * cols, cols), cols)
        right_real = right_ref[0, rows, :]
        right_imag = right_ref[1, rows, :]

        def dot(a, b):
            return lax.dot_general(a, b, NT, preferred_element_type=jnp.float32)

        return (
            dot(phased[0], right_real) - dot(phased[1], right_imag),
            dot(phased[0], right_imag) + dot(phased[1], right_real),
        )

    def x_copy(dest):
        return send(x_out.at[dest], x_in.at[dest], xo_sem.at[dest], xi_sem.at[dest], mate)

    def z_copy(dest, side, site):
        return send(
            z_out.at[dest], z_in.at[dest, side], zo_sem.at[dest], zi_sem.at[dest, side], site
        )

    def first(k, carry):
        dest = order(k, z, nz)
        for part, value in enumerate(partial(dest * PAIR + (1 - x))):
            x_out[dest, part] = value.astype(jnp.bfloat16)
        x_copy(dest).start()
        return carry

    lax.fori_loop(0, nz, first, 0)

    def second(k, carry):
        dest = order(k, z, nz)
        mine = partial(dest * PAIR + x)
        for part in range(2):
            total[part] = mine[part]
        x_copy(dest).wait_recv()
        total[...] += x_in[dest].astype(jnp.float32)

        @pl.when((dest >= z) & has_down)
        def _():
            z_copy(dest, 0, up).wait_recv()
            total[...] += z_in[dest, 0].astype(jnp.float32)

        @pl.when((dest <= z) & has_up)
        def _():
            z_copy(dest, 1, down).wait_recv()
            total[...] += z_in[dest, 1].astype(jnp.float32)

        z_out[dest] = total[...].astype(jnp.bfloat16)

        @pl.when(dest > z)
        def _():
            z_copy(dest, 0, up).start()

        @pl.when(dest < z)
        def _():
            z_copy(dest, 1, down).start()

        return carry

    lax.fori_loop(0, nz, second, 0)

    def block(site):
        return gathered.at[site]

    def to_up(src, site):
        return send(src, block(site), g_up.at[site // PAIR], g_recv.at[site], up)

    def to_down(src, site):
        return send(src, block(site), g_down.at[site // PAIR], g_recv.at[site], down)

    def to_mate(src, site):
        return send(src, block(site), g_pair.at[site // PAIR], g_recv.at[site], mate)

    own = z_out.at[z]

    @pl.when(has_up)
    def _():
        to_up(own, me).start()

    @pl.when(has_down)
    def _():
        to_down(own, me).start()

    to_mate(own, me).start()
    meson_ref[...] = own[...]

    far_copy.wait()

    def gain(value, site):
        rows = pl.ds(pl.multiple_of(site * cols, cols), cols)
        field_real = field[0, rows, :]
        field_imag = field[1, rows, :]

        def dot(a, b):
            return jnp.dot(a, b, preferred_element_type=jnp.float32)

        return (
            dot(value[0], field_real) - dot(value[1], field_imag),
            dot(value[0], field_imag) + dot(value[1], field_real),
        )

    for part, value in enumerate(gain(own, me)):
        total[part] = value

    def arrive(site):
        for part, value in enumerate(gain(block(site), site)):
            total[part] += value

    def relay(d, carry):
        below = me - d * PAIR
        above = me + d * PAIR

        @pl.when(z >= d)
        def _():
            to_up(block(below), below).wait_recv()

            @pl.when(has_up)
            def _():
                to_up(block(below), below).start()

            to_mate(block(below), below).start()

        @pl.when(z + d < nz)
        def _():
            to_down(block(above), above).wait_recv()

            @pl.when(has_down)
            def _():
                to_down(block(above), above).start()

            to_mate(block(above), above).start()

        @pl.when(z >= d)
        def _():
            arrive(below)

        @pl.when(z + d < nz)
        def _():
            arrive(above)

        return carry

    lax.fori_loop(1, nz, relay, 0)

    def across(d, carry):
        @pl.when(z >= d)
        def _():
            site = mate - d * PAIR
            to_mate(block(site), site).wait_recv()
            arrive(site)

        @pl.when((z + d < nz) & (d > 0))
        def _():
            site = mate + d * PAIR
            to_mate(block(site), site).wait_recv()
            arrive(site)

        return carry

    lax.fori_loop(0, nz, across, 0)
    product_ref[...] = total[...].astype(jnp.bfloat16)

    def drain(k, carry):
        x_copy(k).wait_send()

        @pl.when(k != z)
        def _():
            z_copy(k, 0, mate).wait_send()

        to_mate(own, k * PAIR + x).wait_send()

        @pl.when((k <= z) & has_up)
        def _():
            to_up(own, k * PAIR + x).wait_send()

        @pl.when((k >= z) & has_down)
        def _():
            to_down(own, k * PAIR + x).wait_send()

        return carry

    lax.fori_loop(0, nz, drain, 0)


def body(left_modes, right_modes, momenta, far_fields):
    times = lax.axis_size("tm")
    groups = lax.axis_size("site")
    nz = groups // PAIR
    rows, width = left_modes.shape[2:]
    modes, cols = far_fields.shape[2:]
    count = width // SC
    factor = (2.0 * width * groups) ** (-0.5)
    sites = lax.axis_index("site") * count + jnp.arange(count, dtype=jnp.int32)
    momentum = momenta[0]
    coord_x, coord_y, coord_z = block_coords(sites)
    wave = (momentum[0] * coord_x + momentum[1] * coord_y + momentum[2] * coord_z) % EXTENT
    angles = 2.0 * math.pi / EXTENT * wave.astype(jnp.float32)
    waves = jnp.repeat(jnp.stack([jnp.cos(angles), jnp.sin(angles)]), SC, axis=1)
    chunk = (2, rows, cols)
    dma = pltpu.SemaphoreType.DMA
    meson, product = pl.pallas_call(
        functools.partial(kernel, times, groups, factor),
        out_shape=[jax.ShapeDtypeStruct(chunk, jnp.bfloat16)] * 2,
        in_specs=[pl.BlockSpec(memory_space=pltpu.VMEM)] * 3 + [pl.BlockSpec(memory_space=pl.ANY)],
        out_specs=[pl.BlockSpec(memory_space=pltpu.VMEM)] * 2,
        scratch_shapes=[
            pltpu.VMEM((2, rows, width), jnp.bfloat16),
            pltpu.VMEM((2, modes, cols), jnp.bfloat16),
            pltpu.VMEM((nz,) + chunk, jnp.bfloat16),
            pltpu.VMEM((nz,) + chunk, jnp.bfloat16),
            pltpu.VMEM((nz,) + chunk, jnp.bfloat16),
            pltpu.VMEM((nz, 2) + chunk, jnp.bfloat16),
            pltpu.VMEM((groups,) + chunk, jnp.bfloat16),
            pltpu.VMEM(chunk, jnp.float32),
            dma(()),
            dma(()),
            dma((nz,)),
            dma((nz,)),
            dma((nz,)),
            dma((nz, 2)),
            dma((groups,)),
            dma((nz,)),
            dma((nz,)),
            dma((nz,)),
        ],
        compiler_params=pltpu.CompilerParams(
            collective_id=0, has_side_effects=True, vmem_limit_bytes=60 * 2**20
        ),
    )(left_modes[0], right_modes[0], waves, far_fields[0])
    return (meson[None], product[None])


def solution(mesh):
    return jax.shard_map(
        body,
        mesh=mesh,
        in_specs=(
            P("tm", None, None, "site"),
            P("tm", None, None, "site"),
            P("tm", None),
            P("tm", None, None, "site"),
        ),
        out_specs=(P("tm", None, None, "site"), P("tm", None, None, "site")),
        check_vma=False,
    )
```

time: 209 us -> 119 us (0.57)
  Pallas kernels: 0 us -> 104 us
  blocking collectives: 93.4 us -> 0 us
  waiting for transfers between devices: 72 us -> 0 us
  between operations: 14.2 us -> 0.66 us
  local copies, waits for them, and re-layouts: 17.5 us -> 11.6 us
  other arithmetic: 6.78 us -> 2.06 us
  matrix products: 4.58 us -> 0 us
    pallas_call x0 -> x1, Pallas kernels: none -> 104 us  [body(): pl.pallas_call(functools.partial(kernel, times, groups, factor), out_shap...]
    all_to_all x1 -> x0, blocking collectives: 93.4 us -> none  [body(): lax.all_to_all(right_modes[0], 'site', split_axis=1, concat_axis=2, tiled...]
    all_gather x2 -> x0, waiting for transfers between devices: 46.3 us -> none  [the longest x1 46.3 us: body(): shard_piece = lax.all_gather(meson_block, 'site', axis=2, tiled=True)]
    ppermute x1 -> x0, waiting for transfers between devices: 25.7 us -> none  [shifted(): return lax.ppermute(value, axis, pairs)]
    squeeze x3 -> x0, local copies, waits for them, and re-layouts: 4.95 us -> none  [the longest x1 2.72 us: body(): joined = jnp.concatenate([shard_piece[0], shard_piece[1]], axis=1)]
    dot_general x4 -> x0, matrix products: 4.58 us -> none  [the longest x1 1.27 us: body(): jnp.dot(joined, stack_imag, preferred_element_type=jnp.float32)]
    unnamed x7 -> x4, local copies, waits for them, and re-layouts: 5.33 us -> 9.43 us
    all_to_all x1 -> x0, local copies, waits for them, and re-layouts: 3.7 us -> none  [body(): lax.all_to_all(right_modes[0], 'site', split_axis=1, concat_axis=2, tiled...]
  transfers between devices with their start and end apart: 3 -> 0, of which waited for: 2 -> 0; matrix products, arithmetic and copies ran while one was open for 5% -> 0% of each run, Pallas kernels for 0% -> 0%
where the time goes in v1:
time: 119 us
  Pallas kernels  104 us (87%)
  local copies, waits for them, and re-layouts  11.6 us (10%)
  other arithmetic  2.06 us (2%)
    pallas_call x1, Pallas kernels, body(): pl.pallas_call(functools.partial(kernel, times, groups, factor), out_shap...  104 us
    unnamed x4, local copies, waits for them, and re-layouts  9.43 us

profile of v1, /device:TPU:0, one launch (start us, length us, event | category | flops | bytes accessed | tf_op | source)
XLA Modules:
  0.0 118.6 jit_solution(14123461762488286933)
XLA Ops:
  0.6 1.4 %fusion.60 = (s32[1,1]{1,0:T(1,128)}, s32[1,1]{1,0:T(1,128)}, s32[1,1]{1,0:T(1,128)}) fusion(s32[1,3]{1,0:T(1,128)} %param.6), kind=kLoop, calls=%fused_computation.184 | loop fusion | bytes 24 | tf_op jit(solution)/shard_map/slice | solution.py:321
  2.0 2.1 %fusion.58 = (f32[1,16]{1,0:T(1,128)S(1)}, f32[1,16]{1,0:T(1,128)S(1)}) fusion(s32[]{:T(128)} %bitcast.4, s32[]{:T(128)} %bitcast.3, s32[]{:T(128)S(6)} %mul.321, s32[]{:T(128)} %bitcast.2), kind=kLoop, calls=%fused_computation.183 | loop fusion | flops 7664 | bytes 144 | tf_op jit(solution)/shard_map/cos | solution.py:323
  4.2 0.1 broadcast_in_dim.9
  4.2 0.7 reshape.1468.wave_ref
  4.9 2.0 %copy.8 = bf16[1,2,512,192]{3,2,1,0:T(8,128)(2,1)} copy(bf16[1,2,512,192]{2,3,1,0:T(8,128)(2,1)} %param.4) | data formatting | bytes 786432 | tf_op args[0]
  6.9 3.7 %copy.9 = bf16[1,2,2048,192]{3,2,1,0:T(8,128)(2,1)} copy(bf16[1,2,2048,192]{2,3,1,0:T(8,128)(2,1)} %param.5) | data formatting | bytes 3145728 | tf_op args[1]
  10.6 104.3 %shard_map.59 = (bf16[2,512,256]{2,1,0:T(8,128)(2,1)}, bf16[2,512,256]{2,1,0:T(8,128)(2,1)}) custom-call(bf16[2,512,192]{2,1,0:T(8,128)(2,1)} %bitcast.9, bf16[2,2048,192]{2,1,0:T(8,128)(2,1)} %bitcast.8, f32[2,192]{1,0:T(2,128)} %reshape.1468.wave_ref, bf16[2,2048,256]{2,1,0:T(8,128)(2,1)} %bitcast.10), custom_call_target="tpu_custom_call" | custom-call | tf_op jit(solution)/shard_map/pallas_call | solution.py:326
  114.9 1.9 %copy.12 = bf16[1,2,512,256]{3,2,1,0:T(8,128)(2,1)} copy(bf16[1,2,512,256]{3,2,1,0:T(8,128)(2,1)} %bitcast.12) | data formatting | bytes 1048576
  116.7 1.9 %copy.13 = bf16[1,2,512,256]{3,2,1,0:T(8,128)(2,1)} copy(bf16[1,2,512,256]{3,2,1,0:T(8,128)(2,1)} %bitcast.11) | data formatting | bytes 1048576
  (2 shorter events, 0.0 us)

commit v2 on v1

--- a/solution.py
+++ b/solution.py
@@ -13,18 +13,16 @@
 DT = 3
 PAIR = 2
 MESH = pl.DeviceIdType.MESH
-NT = (((1,), (1,)), ((), ()))
 
 
 def block_coords(sites):
-    coord_x = jnp.zeros_like(sites)
-    coord_y = jnp.zeros_like(sites)
-    coord_z = jnp.zeros_like(sites)
-    for level in range(7):
-        coord_x = coord_x + sites // 8**level % 2 * 2**level
-        coord_y = coord_y + sites // (2 * 8**level) % 2 * 2**level
-        coord_z = coord_z + sites // (4 * 8**level) % 2 * 2**level
-    return (coord_x, coord_y, coord_z)
+    coords = []
+    for axis in range(3):
+        coord = jnp.zeros_like(sites)
+        for level in range(7):
+            coord = coord + ((sites >> (3 * level + axis)) & 1) * 2**level
+        coords.append(coord)
+    return coords
 
 
 def order(k, z, nz):
@@ -43,7 +41,7 @@
     factor,
     left_ref,
     right_ref,
-    wave_ref,
+    momenta_ref,
     far_ref,
     meson_ref,
     product_ref,
@@ -65,9 +63,15 @@
     g_up,
     g_down,
     g_pair,
+    s_recv,
+    s_up,
+    s_down,
+    s_pair,
 ):
     nz = groups // PAIR
-    cols = meson_ref.shape[2]
+    rows, cols = meson_ref.shape[1:]
+    width = left_ref.shape[1]
+    thin = max(16, rows // 6 // 16 * 16)
     tm = lax.axis_index("tm")
     me = lax.axis_index("site")
     z = me // PAIR
@@ -115,25 +119,29 @@
     )
     far_copy.start()
 
-    cosine = wave_ref[0:1, :]
-    sine = wave_ref[1:2, :]
+    column = lax.broadcasted_iota(jnp.int32, (width, 128), 0)
+    inside = jnp.floor((column.astype(jnp.float32) + 0.5) / SC).astype(jnp.int32)
+    sites = me * (width // SC) + inside
+    coords = block_coords(sites)
+    wave = sum(momenta_ref[0, axis] * coords[axis] for axis in range(3)).astype(jnp.float32)
+    wave = wave - EXTENT * jnp.floor((wave + 0.5) / EXTENT)
+    angles = 2.0 * math.pi / EXTENT * wave
+    cosine = jnp.cos(angles)[:, 0:1]
+    sine = jnp.sin(angles)[:, 0:1]
     real = left_ref[0].astype(jnp.float32)
     imag = left_ref[1].astype(jnp.float32)
-    phased[0] = (factor * (real * cosine + imag * sine)).astype(jnp.bfloat16)
-    phased[1] = (factor * (real * sine - imag * cosine)).astype(jnp.bfloat16)
+    phased_real = factor * (real * cosine + imag * sine)
+    phased_imag = factor * (real * sine - imag * cosine)
+    for_real = jnp.concatenate([phased_real, -phased_imag], axis=0)
+    for_imag = jnp.concatenate([phased_imag, phased_real], axis=0)
+    phased[0:rows, :] = for_real.T.astype(jnp.bfloat16)
+    phased[rows : 2 * rows, :] = for_imag.T.astype(jnp.bfloat16)
 
     def partial(site):
-        rows = pl.ds(pl.multiple_of(site * cols, cols), cols)
-        right_real = right_ref[0, rows, :]
-        right_imag = right_ref[1, rows, :]
-
-        def dot(a, b):
-            return lax.dot_general(a, b, NT, preferred_element_type=jnp.float32)
-
-        return (
-            dot(phased[0], right_real) - dot(phased[1], right_imag),
-            dot(phased[0], right_imag) + dot(phased[1], right_real),
-        )
+        lanes = pl.ds(pl.multiple_of(site * cols, cols), cols)
+        right = right_ref[:, :, lanes].reshape(2 * width, cols)
+        both = jnp.dot(phased[...], right, preferred_element_type=jnp.float32)
+        return both.reshape(2, rows, cols)
 
     def x_copy(dest):
         return send(x_out.at[dest], x_in.at[dest], xo_sem.at[dest], xi_sem.at[dest], mate)
@@ -145,8 +153,7 @@
 
     def first(k, carry):
         dest = order(k, z, nz)
-        for part, value in enumerate(partial(dest * PAIR + (1 - x))):
-            x_out[dest, part] = value.astype(jnp.bfloat16)
+        x_out[dest] = partial(dest * PAIR + (1 - x)).astype(jnp.bfloat16)
         x_copy(dest).start()
         return carry
 
@@ -154,9 +161,7 @@
 
     def second(k, carry):
         dest = order(k, z, nz)
-        mine = partial(dest * PAIR + x)
-        for part in range(2):
-            total[part] = mine[part]
+        total[...] = partial(dest * PAIR + x)
         x_copy(dest).wait_recv()
         total[...] += x_in[dest].astype(jnp.float32)
 
@@ -193,10 +198,30 @@
     def to_down(src, site):
         return send(src, block(site), g_down.at[site // PAIR], g_recv.at[site], down)
 
+    def slim(ref):
+        return ref.at[:, pl.ds(0, thin), :]
+
+    def rest(ref):
+        return ref.at[:, pl.ds(thin, rows - thin), :]
+
     def to_mate(src, site):
-        return send(src, block(site), g_pair.at[site // PAIR], g_recv.at[site], mate)
+        return send(
+            rest(src), rest(block(site)), g_pair.at[site // PAIR], g_recv.at[site], mate
+        )
+
+    def slim_up(site):
+        part = slim(block(site))
+        return send(part, part, s_up.at[site // PAIR], s_recv.at[site], up)
+
+    def slim_down(site):
+        part = slim(block(site))
+        return send(part, part, s_down.at[site // PAIR], s_recv.at[site], down)
+
+    def slim_mate(src, site):
+        return send(slim(src), slim(block(site)), s_pair, s_recv.at[site], mate)
 
     own = z_out.at[z]
+    slim_mate(own, me).start()
 
     @pl.when(has_up)
     def _():
@@ -208,21 +233,29 @@
 
     to_mate(own, me).start()
     meson_ref[...] = own[...]
+    slim_mate(block(mate), mate).wait_recv()
+
+    @pl.when(has_up)
+    def _():
+        slim_up(mate).start()
+
+    @pl.when(has_down)
+    def _():
+        slim_down(mate).start()
 
     far_copy.wait()
 
     def gain(value, site):
-        rows = pl.ds(pl.multiple_of(site * cols, cols), cols)
-        field_real = field[0, rows, :]
-        field_imag = field[1, rows, :]
-
-        def dot(a, b):
-            return jnp.dot(a, b, preferred_element_type=jnp.float32)
-
-        return (
-            dot(value[0], field_real) - dot(value[1], field_imag),
-            dot(value[0], field_imag) + dot(value[1], field_real),
-        )
+        lines = pl.ds(pl.multiple_of(site * cols, cols), cols)
+        both = value[...].reshape(2 * rows, cols)
+
+        def dot(part):
+            whole = jnp.dot(both, field[part, lines, :], preferred_element_type=jnp.float32)
+            return whole[:rows], whole[rows:]
+
+        real_real, imag_real = dot(0)
+        real_imag, imag_imag = dot(1)
+        return (real_real - imag_imag, real_imag + imag_real)
 
     for part, value in enumerate(gain(own, me)):
         total[part] = value
@@ -263,6 +296,24 @@
         def _():
             arrive(above)
 
+        @pl.when(z >= d)
+        def _():
+            site = mate - d * PAIR
+            slim_up(site).wait_recv()
+
+            @pl.when(has_up)
+            def _():
+                slim_up(site).start()
+
+        @pl.when(z + d < nz)
+        def _():
+            site = mate + d * PAIR
+            slim_down(site).wait_recv()
+
+            @pl.when(has_down)
+            def _():
+                slim_down(site).start()
+
         return carry
 
     lax.fori_loop(1, nz, relay, 0)
@@ -297,14 +348,22 @@
         @pl.when((k <= z) & has_up)
         def _():
             to_up(own, k * PAIR + x).wait_send()
+            slim_up(k * PAIR + 1 - x).wait_send()
 
         @pl.when((k >= z) & has_down)
         def _():
             to_down(own, k * PAIR + x).wait_send()
+            slim_down(k * PAIR + 1 - x).wait_send()
 
         return carry
 
     lax.fori_loop(0, nz, drain, 0)
+    slim_mate(own, me).wait_send()
+
+
+def settle(meson_in, product_in, meson_ref, product_ref):
+    meson_ref[...] = meson_in[...]
+    product_ref[...] = product_in[...]
 
 
 def body(left_modes, right_modes, momenta, far_fields):
@@ -313,23 +372,21 @@
     nz = groups // PAIR
     rows, width = left_modes.shape[2:]
     modes, cols = far_fields.shape[2:]
-    count = width // SC
     factor = (2.0 * width * groups) ** (-0.5)
-    sites = lax.axis_index("site") * count + jnp.arange(count, dtype=jnp.int32)
-    momentum = momenta[0]
-    coord_x, coord_y, coord_z = block_coords(sites)
-    wave = (momentum[0] * coord_x + momentum[1] * coord_y + momentum[2] * coord_z) % EXTENT
-    angles = 2.0 * math.pi / EXTENT * wave.astype(jnp.float32)
-    waves = jnp.repeat(jnp.stack([jnp.cos(angles), jnp.sin(angles)]), SC, axis=1)
     chunk = (2, rows, cols)
     dma = pltpu.SemaphoreType.DMA
     meson, product = pl.pallas_call(
         functools.partial(kernel, times, groups, factor),
         out_shape=[jax.ShapeDtypeStruct(chunk, jnp.bfloat16)] * 2,
-        in_specs=[pl.BlockSpec(memory_space=pltpu.VMEM)] * 3 + [pl.BlockSpec(memory_space=pl.ANY)],
+        in_specs=[
+            pl.BlockSpec(memory_space=pltpu.VMEM),
+            pl.BlockSpec(memory_space=pltpu.VMEM),
+            pl.BlockSpec(memory_space=pltpu.SMEM),
+            pl.BlockSpec(memory_space=pl.ANY),
+        ],
         out_specs=[pl.BlockSpec(memory_space=pltpu.VMEM)] * 2,
         scratch_shapes=[
-            pltpu.VMEM((2, rows, width), jnp.bfloat16),
+            pltpu.VMEM((2 * rows, 2 * width), jnp.bfloat16),
             pltpu.VMEM((2, modes, cols), jnp.bfloat16),
             pltpu.VMEM((nz,) + chunk, jnp.bfloat16),
             pltpu.VMEM((nz,) + chunk, jnp.bfloat16),
@@ -347,11 +404,27 @@
             dma((nz,)),
             dma((nz,)),
             dma((nz,)),
+            dma((groups,)),
+            dma((nz,)),
+            dma((nz,)),
+            dma(()),
         ],
         compiler_params=pltpu.CompilerParams(
             collective_id=0, has_side_effects=True, vmem_limit_bytes=60 * 2**20
         ),
-    )(left_modes[0], right_modes[0], waves, far_fields[0])
+    )(
+        jnp.swapaxes(left_modes[0], 1, 2),
+        jnp.swapaxes(right_modes[0], 1, 2),
+        momenta,
+        far_fields[0],
+    )
+    meson, product = pl.pallas_call(
+        settle,
+        out_shape=[jax.ShapeDtypeStruct(chunk, jnp.bfloat16)] * 2,
+        in_specs=[pl.BlockSpec(memory_space=pltpu.VMEM)] * 2,
+        out_specs=[pl.BlockSpec(memory_space=pltpu.VMEM)] * 2,
+        compiler_params=pltpu.CompilerParams(vmem_limit_bytes=16 * 2**20),
+    )(meson, product)
     return (meson[None], product[None])
 
 

time: 119 us -> 111 us (0.933)
  local copies, waits for them, and re-layouts: 11.6 us -> 2.08 us
  Pallas kernels: 104 us -> 107 us
  other arithmetic: 2.06 us -> 0 us
    unnamed x4, local copies, waits for them, and re-layouts: 9.43 us -> 2.08 us
    pallas_call x1, Pallas kernels: 104 us -> 106 us  [body(): pl.pallas_call(functools.partial(kernel, times, groups, factor), out_shap...]
    cos x1 -> x0, other arithmetic: 2.05 us -> none  [body(): jnp.cos(angles)]
    slice x1 -> x0, local copies, waits for them, and re-layouts: 1.42 us -> none  [body(): momentum[0] * coord_x + momentum[1] * coord_y + momentum[2] * coord_z]
where the time goes in v2:
time: 111 us; the launch traced here: 110 us
  Pallas kernels  107 us (96%)
  local copies, waits for them, and re-layouts  2.08 us (2%)
    pallas_call x1, Pallas kernels, body(): pl.pallas_call(functools.partial(kernel, times, groups, factor), out_shap...  106 us

profile of v2, /device:TPU:0, one launch (start us, length us, event | category | flops | bytes accessed | tf_op | source)
XLA Modules:
  0.0 110.2 jit_solution(14968647383042445867)
XLA Ops:
  0.6 106.4 %shard_map.59 = (bf16[2,512,256]{2,1,0:T(8,128)(2,1)}, bf16[2,512,256]{2,1,0:T(8,128)(2,1)}) custom-call(bf16[2,192,512]{2,1,0:T(8,128)(2,1)} %bitcast.11, bf16[2,192,2048]{2,1,0:T(8,128)(2,1)} %bitcast.10, s32[1,3]{1,0:T(1,128)} %momenta_ref.1, bf16[2,2048,256]{2,1,0:T(8,128)(2,1)} %bitcast.9), custom_call_target="tpu_custom_call" | custom-call | tf_op jit(solution)/shard_map/pallas_call | solution.py:378
  107.1 0.0 copy-start
  107.1 1.0 copy-done
  108.1 0.0 copy-start.1
  108.1 1.0 copy-done.1
  109.2 1.0 shard_map.60
Async XLA Ops:
  107.1 1.0 copy-start
  108.1 1.0 copy-start.1

commit v3 on v2

--- a/solution.py
+++ b/solution.py
@@ -23,6 +23,10 @@
             coord = coord + ((sites >> (3 * level + axis)) & 1) * 2**level
         coords.append(coord)
     return coords
+
+
+def thin_rows(rows):
+    return max(16, rows // 6 // 16 * 16)
 
 
 def order(k, z, nz):
@@ -67,11 +71,24 @@
     s_up,
     s_down,
     s_pair,
+    left_in,
+    right_in,
+    left_sem,
+    right_sem,
+    kept,
+    t_out,
+    t_in,
+    to_sem,
+    ti_sem,
+    m_out,
+    m_in,
+    m_sem,
+    mine,
 ):
     nz = groups // PAIR
     rows, cols = meson_ref.shape[1:]
     width = left_ref.shape[1]
-    thin = max(16, rows // 6 // 16 * 16)
+    thin = thin_rows(rows)
     tm = lax.axis_index("tm")
     me = lax.axis_index("site")
     z = me // PAIR
@@ -84,6 +101,21 @@
     target = lax.rem(tm + times - DT % times, times)
     source = lax.rem(tm + DT, times)
 
+    left_copy = pltpu.make_async_copy(left_ref, left_in, left_sem)
+    left_copy.start()
+
+    def right_copy(site):
+        lanes = pl.ds(pl.multiple_of(site * cols, cols), cols)
+        return pltpu.make_async_copy(right_ref.at[:, :, lanes], right_in.at[site], right_sem.at[site])
+
+    def load(k, carry):
+        dest = order(k, z, nz)
+        right_copy(dest * PAIR + (1 - x)).start()
+        right_copy(dest * PAIR + x).start()
+        return carry
+
+    lax.fori_loop(0, nz, load, 0)
+
     barrier = pltpu.get_barrier_semaphore()
     pl.semaphore_signal(barrier, inc=1, device_id=(target, me), device_id_type=MESH)
     pl.semaphore_signal(barrier, inc=1, device_id=(source, me), device_id_type=MESH)
@@ -96,8 +128,6 @@
     @pl.when(has_down)
     def _():
         pl.semaphore_signal(barrier, inc=1, device_id=(tm, down), device_id_type=MESH)
-
-    pl.semaphore_wait(barrier, 3 + has_up.astype(jnp.int32) + has_down.astype(jnp.int32))
 
     def send(src, dst, send_sem, recv_sem, site):
         return pltpu.make_async_remote_copy(
@@ -109,6 +139,27 @@
             device_id_type=MESH,
         )
 
+    column = lax.broadcasted_iota(jnp.int32, (width, 128), 0)
+    inside = jnp.floor((column.astype(jnp.float32) + 0.5) / SC).astype(jnp.int32)
+    sites = me * (width // SC) + inside
+    coords = block_coords(sites)
+    wave = sum(momenta_ref[0, axis] * coords[axis] for axis in range(3)).astype(jnp.float32)
+    wave = wave - EXTENT * jnp.floor((wave + 0.5) / EXTENT)
+    angles = 2.0 * math.pi / EXTENT * wave
+    cosine = jnp.cos(angles)[:, 0:1]
+    sine = jnp.sin(angles)[:, 0:1]
+    left_copy.wait()
+    real = left_in[0].astype(jnp.float32)
+    imag = left_in[1].astype(jnp.float32)
+    phased_real = factor * (real * cosine + imag * sine)
+    phased_imag = factor * (real * sine - imag * cosine)
+    for_real = jnp.concatenate([phased_real, -phased_imag], axis=0)
+    for_imag = jnp.concatenate([phased_imag, phased_real], axis=0)
+    phased[0:rows, :] = for_real.T.astype(jnp.bfloat16)
+    phased[rows : 2 * rows, :] = for_imag.T.astype(jnp.bfloat16)
+
+    pl.semaphore_wait(barrier, 3 + has_up.astype(jnp.int32) + has_down.astype(jnp.int32))
+
     far_copy = pltpu.make_async_remote_copy(
         src_ref=far_ref,
         dst_ref=field,
@@ -119,27 +170,9 @@
     )
     far_copy.start()
 
-    column = lax.broadcasted_iota(jnp.int32, (width, 128), 0)
-    inside = jnp.floor((column.astype(jnp.float32) + 0.5) / SC).astype(jnp.int32)
-    sites = me * (width // SC) + inside
-    coords = block_coords(sites)
-    wave = sum(momenta_ref[0, axis] * coords[axis] for axis in range(3)).astype(jnp.float32)
-    wave = wave - EXTENT * jnp.floor((wave + 0.5) / EXTENT)
-    angles = 2.0 * math.pi / EXTENT * wave
-    cosine = jnp.cos(angles)[:, 0:1]
-    sine = jnp.sin(angles)[:, 0:1]
-    real = left_ref[0].astype(jnp.float32)
-    imag = left_ref[1].astype(jnp.float32)
-    phased_real = factor * (real * cosine + imag * sine)
-    phased_imag = factor * (real * sine - imag * cosine)
-    for_real = jnp.concatenate([phased_real, -phased_imag], axis=0)
-    for_imag = jnp.concatenate([phased_imag, phased_real], axis=0)
-    phased[0:rows, :] = for_real.T.astype(jnp.bfloat16)
-    phased[rows : 2 * rows, :] = for_imag.T.astype(jnp.bfloat16)
-
     def partial(site):
-        lanes = pl.ds(pl.multiple_of(site * cols, cols), cols)
-        right = right_ref[:, :, lanes].reshape(2 * width, cols)
+        right_copy(site).wait()
+        right = right_in[site].reshape(2 * width, cols)
         both = jnp.dot(phased[...], right, preferred_element_type=jnp.float32)
         return both.reshape(2, rows, cols)
 
@@ -151,43 +184,91 @@
             z_out.at[dest], z_in.at[dest, side], zo_sem.at[dest], zi_sem.at[dest, side], site
         )
 
+    def t_copy(dest, side, site):
+        return send(
+            t_out.at[dest], t_in.at[dest, side], to_sem.at[dest], ti_sem.at[dest, side], site
+        )
+
+    m_copy = send(m_out, m_in, m_sem.at[0], m_sem.at[1], mate)
+
     def first(k, carry):
         dest = order(k, z, nz)
-        x_out[dest] = partial(dest * PAIR + (1 - x)).astype(jnp.bfloat16)
+        theirs = partial(dest * PAIR + (1 - x))
+        x_out[dest] = theirs[:, thin:].astype(jnp.bfloat16)
         x_copy(dest).start()
+        kept[dest, 1, :, :thin] = theirs[:, :thin]
+        kept[dest, 0] = partial(dest * PAIR + x)
+
+        @pl.when((dest > z) & has_down)
+        def _():
+            t_copy(dest, 0, up).wait_recv()
+            kept[dest, :, :, :thin] += t_in[dest, 0].astype(jnp.float32)
+
+        @pl.when((dest < z) & has_up)
+        def _():
+            t_copy(dest, 1, down).wait_recv()
+            kept[dest, :, :, :thin] += t_in[dest, 1].astype(jnp.float32)
+
+        @pl.when(dest > z)
+        def _():
+            t_out[dest] = kept[dest, :, :, :thin].astype(jnp.bfloat16)
+            t_copy(dest, 0, up).start()
+
+        @pl.when(dest < z)
+        def _():
+            t_out[dest] = kept[dest, :, :, :thin].astype(jnp.bfloat16)
+            t_copy(dest, 1, down).start()
+
         return carry
 
     lax.fori_loop(0, nz, first, 0)
 
     def second(k, carry):
         dest = order(k, z, nz)
-        total[...] = partial(dest * PAIR + x)
         x_copy(dest).wait_recv()
-        total[...] += x_in[dest].astype(jnp.float32)
+        kept[dest, 0, :, thin:] += x_in[dest].astype(jnp.float32)
 
         @pl.when((dest >= z) & has_down)
         def _():
             z_copy(dest, 0, up).wait_recv()
-            total[...] += z_in[dest, 0].astype(jnp.float32)
+            kept[dest, 0, :, thin:] += z_in[dest, 0].astype(jnp.float32)
 
         @pl.when((dest <= z) & has_up)
         def _():
             z_copy(dest, 1, down).wait_recv()
-            total[...] += z_in[dest, 1].astype(jnp.float32)
-
-        z_out[dest] = total[...].astype(jnp.bfloat16)
+            kept[dest, 0, :, thin:] += z_in[dest, 1].astype(jnp.float32)
 
         @pl.when(dest > z)
         def _():
+            z_out[dest] = kept[dest, 0, :, thin:].astype(jnp.bfloat16)
             z_copy(dest, 0, up).start()
 
         @pl.when(dest < z)
         def _():
+            z_out[dest] = kept[dest, 0, :, thin:].astype(jnp.bfloat16)
             z_copy(dest, 1, down).start()
 
+        @pl.when(k == 0)
+        def _():
+            @pl.when(has_down)
+            def _():
+                t_copy(z, 0, up).wait_recv()
+                kept[z, :, :, :thin] += t_in[z, 0].astype(jnp.float32)
+
+            @pl.when(has_up)
+            def _():
+                t_copy(z, 1, down).wait_recv()
+                kept[z, :, :, :thin] += t_in[z, 1].astype(jnp.float32)
+
+            m_out[...] = kept[z, 1, :, :thin].astype(jnp.bfloat16)
+            m_copy.start()
+
         return carry
 
     lax.fori_loop(0, nz, second, 0)
+    m_copy.wait_recv()
+    kept[z, 0, :, :thin] += m_in[...].astype(jnp.float32)
+    mine[...] = kept[z, 0].astype(jnp.bfloat16)
 
     def block(site):
         return gathered.at[site]
@@ -220,7 +301,7 @@
     def slim_mate(src, site):
         return send(slim(src), slim(block(site)), s_pair, s_recv.at[site], mate)
 
-    own = z_out.at[z]
+    own = mine
     slim_mate(own, me).start()
 
     @pl.when(has_up)
@@ -342,6 +423,7 @@
         @pl.when(k != z)
         def _():
             z_copy(k, 0, mate).wait_send()
+            t_copy(k, 0, mate).wait_send()
 
         to_mate(own, k * PAIR + x).wait_send()
 
@@ -359,11 +441,25 @@
 
     lax.fori_loop(0, nz, drain, 0)
     slim_mate(own, me).wait_send()
-
-
-def settle(meson_in, product_in, meson_ref, product_ref):
-    meson_ref[...] = meson_in[...]
-    product_ref[...] = product_in[...]
+    m_copy.wait_send()
+
+
+def settle(meson_in, product_in, meson_ref, product_ref, held, in_sem, out_sem):
+    parts = meson_in.shape[0]
+    pairs = [(meson_in, meson_ref), (product_in, product_ref)]
+    into, out = [], []
+    for which, (src, dst) in enumerate(pairs):
+        for part in range(parts):
+            slot = which * parts + part
+            into.append(pltpu.make_async_copy(src.at[part], held.at[slot], in_sem.at[slot]))
+            out.append(pltpu.make_async_copy(held.at[slot], dst.at[part], out_sem.at[slot]))
+    for copy in into:
+        copy.start()
+    for arrived, copy in zip(into, out):
+        arrived.wait()
+        copy.start()
+    for copy in out:
+        copy.wait()
 
 
 def body(left_modes, right_modes, momenta, far_fields):
@@ -374,13 +470,16 @@
     modes, cols = far_fields.shape[2:]
     factor = (2.0 * width * groups) ** (-0.5)
     chunk = (2, rows, cols)
+    thin = thin_rows(rows)
+    large = (2, rows - thin, cols)
+    small = (2, thin, cols)
     dma = pltpu.SemaphoreType.DMA
     meson, product = pl.pallas_call(
         functools.partial(kernel, times, groups, factor),
         out_shape=[jax.ShapeDtypeStruct(chunk, jnp.bfloat16)] * 2,
         in_specs=[
-            pl.BlockSpec(memory_space=pltpu.VMEM),
-            pl.BlockSpec(memory_space=pltpu.VMEM),
+            pl.BlockSpec(memory_space=pl.ANY),
+            pl.BlockSpec(memory_space=pl.ANY),
             pl.BlockSpec(memory_space=pltpu.SMEM),
             pl.BlockSpec(memory_space=pl.ANY),
         ],
@@ -388,10 +487,10 @@
         scratch_shapes=[
             pltpu.VMEM((2 * rows, 2 * width), jnp.bfloat16),
             pltpu.VMEM((2, modes, cols), jnp.bfloat16),
-            pltpu.VMEM((nz,) + chunk, jnp.bfloat16),
-            pltpu.VMEM((nz,) + chunk, jnp.bfloat16),
-            pltpu.VMEM((nz,) + chunk, jnp.bfloat16),
-            pltpu.VMEM((nz, 2) + chunk, jnp.bfloat16),
+            pltpu.VMEM((nz,) + large, jnp.bfloat16),
+            pltpu.VMEM((nz,) + large, jnp.bfloat16),
+            pltpu.VMEM((nz,) + large, jnp.bfloat16),
+            pltpu.VMEM((nz, 2) + large, jnp.bfloat16),
             pltpu.VMEM((groups,) + chunk, jnp.bfloat16),
             pltpu.VMEM(chunk, jnp.float32),
             dma(()),
@@ -408,6 +507,19 @@
             dma((nz,)),
             dma((nz,)),
             dma(()),
+            pltpu.VMEM((2, width, rows), jnp.bfloat16),
+            pltpu.VMEM((groups, 2, width, cols), jnp.bfloat16),
+            dma(()),
+            dma((groups,)),
+            pltpu.VMEM((nz, PAIR) + chunk, jnp.float32),
+            pltpu.VMEM((nz, PAIR) + small, jnp.bfloat16),
+            pltpu.VMEM((nz, 2, PAIR) + small, jnp.bfloat16),
+            dma((nz,)),
+            dma((nz, 2)),
+            pltpu.VMEM(small, jnp.bfloat16),
+            pltpu.VMEM(small, jnp.bfloat16),
+            dma((2,)),
+            pltpu.VMEM(chunk, jnp.bfloat16),
         ],
         compiler_params=pltpu.CompilerParams(
             collective_id=0, has_side_effects=True, vmem_limit_bytes=60 * 2**20
@@ -421,9 +533,10 @@
     meson, product = pl.pallas_call(
         settle,
         out_shape=[jax.ShapeDtypeStruct(chunk, jnp.bfloat16)] * 2,
-        in_specs=[pl.BlockSpec(memory_space=pltpu.VMEM)] * 2,
-        out_specs=[pl.BlockSpec(memory_space=pltpu.VMEM)] * 2,
-        compiler_params=pltpu.CompilerParams(vmem_limit_bytes=16 * 2**20),
+        in_specs=[pl.BlockSpec(memory_space=pl.ANY)] * 2,
+        out_specs=[pl.BlockSpec(memory_space=pl.ANY)] * 2,
+        scratch_shapes=[pltpu.VMEM((4, rows, cols), jnp.bfloat16), dma((4,)), dma((4,))],
+        compiler_params=pltpu.CompilerParams(vmem_limit_bytes=60 * 2**20),
     )(meson, product)
     return (meson[None], product[None])
 

time: 111 us -> 101 us (0.910)
  Pallas kernels: 107 us -> 100 us
  local copies, waits for them, and re-layouts: 2.08 us -> 0 us
    pallas_call x1, Pallas kernels: 106 us -> 98.3 us  [body(): pl.pallas_call(functools.partial(kernel, times, groups, factor), out_shap...]
    unnamed x4 -> x0, local copies, waits for them, and re-layouts: 2.08 us -> none
where the time goes in v3:
time: 101 us
  Pallas kernels  100 us (99%)
    pallas_call x1, Pallas kernels, body(): pl.pallas_call(functools.partial(kernel, times, groups, factor), out_shap...  98.3 us

profile of v3, /device:TPU:0, one launch (start us, length us, event | category | flops | bytes accessed | tf_op | source)
XLA Modules:
  0.0 100.9 jit_solution(10439200691067173792)
XLA Ops:
  0.6 98.3 %shard_map.59 = (bf16[2,512,256]{2,1,0:T(8,128)(2,1)}, bf16[2,512,256]{2,1,0:T(8,128)(2,1)}) custom-call(bf16[2,192,512]{2,1,0:T(8,128)(2,1)} %bitcast.11, bf16[2,192,2048]{2,1,0:T(8,128)(2,1)} %bitcast.10, s32[1,3]{1,0:T(1,128)} %momenta_ref.1, bf16[2,2048,256]{2,1,0:T(8,128)(2,1)} %bitcast.9), custom_call_target="tpu_custom_call" | custom-call | tf_op jit(solution)/shard_map/pallas_call | solution.py:477
  98.9 2.0 %shard_map.60 = (bf16[2,512,256]{2,1,0:T(8,128)(2,1)}, bf16[2,512,256]{2,1,0:T(8,128)(2,1)}) custom-call(bf16[2,512,256]{2,1,0:T(8,128)(2,1)} %get-tuple-element.6.meson_in, bf16[2,512,256]{2,1,0:T(8,128)(2,1)} %get-tuple-element.7.product_in), custom_call_target="tpu_custom_call" | custom-call | tf_op jit(solution)/shard_map/pallas_call | solution.py:533

commit v4 on v3

--- a/solution.py
+++ b/solution.py
@@ -83,7 +83,8 @@
     m_out,
     m_in,
     m_sem,
-    mine,
+    staged,
+    leave,
 ):
     nz = groups // PAIR
     rows, cols = meson_ref.shape[1:]
@@ -268,61 +269,65 @@
     lax.fori_loop(0, nz, second, 0)
     m_copy.wait_recv()
     kept[z, 0, :, :thin] += m_in[...].astype(jnp.float32)
-    mine[...] = kept[z, 0].astype(jnp.bfloat16)
+    gathered[me] = kept[z, 0].astype(jnp.bfloat16)
 
     def block(site):
         return gathered.at[site]
 
-    def to_up(src, site):
-        return send(src, block(site), g_up.at[site // PAIR], g_recv.at[site], up)
-
-    def to_down(src, site):
-        return send(src, block(site), g_down.at[site // PAIR], g_recv.at[site], down)
-
     def slim(ref):
         return ref.at[:, pl.ds(0, thin), :]
 
-    def rest(ref):
-        return ref.at[:, pl.ds(thin, rows - thin), :]
-
-    def to_mate(src, site):
-        return send(
-            rest(src), rest(block(site)), g_pair.at[site // PAIR], g_recv.at[site], mate
-        )
+    def rest(site):
+        return gathered.at[site, :, pl.ds(thin, rows - thin), :]
+
+    def pair(site):
+        first_of = pl.multiple_of(site // PAIR * PAIR, PAIR)
+        return gathered.at[pl.ds(first_of, PAIR), :, pl.ds(0, thin), :]
+
+    def to_up(site):
+        return send(rest(site), rest(site), g_up.at[site // PAIR], g_recv.at[site], up)
+
+    def to_down(site):
+        return send(rest(site), rest(site), g_down.at[site // PAIR], g_recv.at[site], down)
+
+    def to_mate(site):
+        return send(rest(site), rest(site), g_pair.at[site // PAIR], g_recv.at[site], mate)
 
     def slim_up(site):
-        part = slim(block(site))
-        return send(part, part, s_up.at[site // PAIR], s_recv.at[site], up)
+        line = site // PAIR
+        return send(pair(site), pair(site), s_up.at[line], s_recv.at[line], up)
 
     def slim_down(site):
-        part = slim(block(site))
-        return send(part, part, s_down.at[site // PAIR], s_recv.at[site], down)
-
-    def slim_mate(src, site):
-        return send(slim(src), slim(block(site)), s_pair, s_recv.at[site], mate)
-
-    own = mine
-    slim_mate(own, me).start()
+        line = site // PAIR
+        return send(pair(site), pair(site), s_down.at[line], s_recv.at[line], down)
+
+    def slim_mate(site):
+        return send(slim(block(site)), slim(block(site)), s_pair, s_recv.at[z], mate)
+
+    own = block(me)
 
     @pl.when(has_up)
     def _():
-        to_up(own, me).start()
+        to_up(me).start()
 
     @pl.when(has_down)
     def _():
-        to_down(own, me).start()
-
-    to_mate(own, me).start()
-    meson_ref[...] = own[...]
-    slim_mate(block(mate), mate).wait_recv()
-
-    @pl.when(has_up)
+        to_down(me).start()
+
+    slim_mate(me).start()
+    to_mate(me).start()
+    meson_copy = pltpu.make_async_copy(own, meson_ref, leave.at[0])
+    meson_copy.start()
+
+    slim_mate(mate).wait_recv()
+
+    @pl.when((z == 0) & has_up)
     def _():
-        slim_up(mate).start()
-
-    @pl.when(has_down)
+        slim_up(me).start()
+
+    @pl.when((z == nz - 1) & has_down)
     def _():
-        slim_down(mate).start()
+        slim_down(me).start()
 
     far_copy.wait()
 
@@ -351,71 +356,90 @@
 
         @pl.when(z >= d)
         def _():
-            to_up(block(below), below).wait_recv()
+            to_up(below).wait_recv()
 
             @pl.when(has_up)
             def _():
-                to_up(block(below), below).start()
-
-            to_mate(block(below), below).start()
+                to_up(below).start()
+
+            to_mate(below).start()
+
+        @pl.when((z == d) & has_up)
+        def _():
+            slim_up(me).start()
 
         @pl.when(z + d < nz)
         def _():
-            to_down(block(above), above).wait_recv()
+            to_down(above).wait_recv()
 
             @pl.when(has_down)
             def _():
-                to_down(block(above), above).start()
-
-            to_mate(block(above), above).start()
+                to_down(above).start()
+
+            to_mate(above).start()
+
+        @pl.when((z + d == nz - 1) & has_down)
+        def _():
+            slim_down(me).start()
+
+        return carry
+
+    lax.fori_loop(1, nz, relay, 0)
+
+    def thins(d, carry):
+        below = me - d * PAIR
+        above = me + d * PAIR
 
         @pl.when(z >= d)
         def _():
-            arrive(below)
-
-        @pl.when(z + d < nz)
-        def _():
-            arrive(above)
-
-        @pl.when(z >= d)
-        def _():
-            site = mate - d * PAIR
-            slim_up(site).wait_recv()
+            slim_up(below).wait_recv()
 
             @pl.when(has_up)
             def _():
-                slim_up(site).start()
+                slim_up(below).start()
 
         @pl.when(z + d < nz)
         def _():
-            site = mate + d * PAIR
-            slim_down(site).wait_recv()
+            slim_down(above).wait_recv()
 
             @pl.when(has_down)
             def _():
-                slim_down(site).start()
-
-        return carry
-
-    lax.fori_loop(1, nz, relay, 0)
+                slim_down(above).start()
+
+        @pl.when(z >= d)
+        def _():
+            arrive(below)
+
+        @pl.when(z + d < nz)
+        def _():
+            arrive(above)
+
+        return carry
+
+    lax.fori_loop(1, nz, thins, 0)
 
     def across(d, carry):
         @pl.when(z >= d)
         def _():
             site = mate - d * PAIR
-            to_mate(block(site), site).wait_recv()
+            to_mate(site).wait_recv()
             arrive(site)
 
         @pl.when((z + d < nz) & (d > 0))
         def _():
             site = mate + d * PAIR
-            to_mate(block(site), site).wait_recv()
+            to_mate(site).wait_recv()
             arrive(site)
 
         return carry
 
     lax.fori_loop(0, nz, across, 0)
-    product_ref[...] = total[...].astype(jnp.bfloat16)
+    copies = [meson_copy]
+    for part in range(2):
+        staged[part] = total[part].astype(jnp.bfloat16)
+        copy = pltpu.make_async_copy(staged.at[part], product_ref.at[part], leave.at[1 + part])
+        copy.start()
+        copies.append(copy)
 
     def drain(k, carry):
         x_copy(k).wait_send()
@@ -425,23 +449,25 @@
             z_copy(k, 0, mate).wait_send()
             t_copy(k, 0, mate).wait_send()
 
-        to_mate(own, k * PAIR + x).wait_send()
+        to_mate(k * PAIR + x).wait_send()
 
         @pl.when((k <= z) & has_up)
         def _():
-            to_up(own, k * PAIR + x).wait_send()
-            slim_up(k * PAIR + 1 - x).wait_send()
+            to_up(k * PAIR + x).wait_send()
+            slim_up(k * PAIR).wait_send()
 
         @pl.when((k >= z) & has_down)
         def _():
-            to_down(own, k * PAIR + x).wait_send()
-            slim_down(k * PAIR + 1 - x).wait_send()
+            to_down(k * PAIR + x).wait_send()
+            slim_down(k * PAIR).wait_send()
 
         return carry
 
     lax.fori_loop(0, nz, drain, 0)
-    slim_mate(own, me).wait_send()
+    slim_mate(me).wait_send()
     m_copy.wait_send()
+    for copy in copies:
+        copy.wait()
 
 
 def settle(meson_in, product_in, meson_ref, product_ref, held, in_sem, out_sem):
@@ -483,7 +509,7 @@
             pl.BlockSpec(memory_space=pltpu.SMEM),
             pl.BlockSpec(memory_space=pl.ANY),
         ],
-        out_specs=[pl.BlockSpec(memory_space=pltpu.VMEM)] * 2,
+        out_specs=[pl.BlockSpec(memory_space=pl.ANY)] * 2,
         scratch_shapes=[
             pltpu.VMEM((2 * rows, 2 * width), jnp.bfloat16),
             pltpu.VMEM((2, modes, cols), jnp.bfloat16),
@@ -503,7 +529,7 @@
             dma((nz,)),
             dma((nz,)),
             dma((nz,)),
-            dma((groups,)),
+            dma((nz,)),
             dma((nz,)),
             dma((nz,)),
             dma(()),
@@ -520,6 +546,7 @@
             pltpu.VMEM(small, jnp.bfloat16),
             dma((2,)),
             pltpu.VMEM(chunk, jnp.bfloat16),
+            dma((3,)),
         ],
         compiler_params=pltpu.CompilerParams(
             collective_id=0, has_side_effects=True, vmem_limit_bytes=60 * 2**20

time: 101 us -> 96.4 us (0.954)
  Pallas kernels: 100 us -> 95.6 us
    pallas_call x1, Pallas kernels: 98.3 us -> 93.6 us  [body(): pl.pallas_call(functools.partial(kernel, times, groups, factor), out_shap...]
where the time goes in v4:
time: 96.4 us; the launch traced here: 96.3 us
  Pallas kernels  95.6 us (99%)
    pallas_call x1, Pallas kernels, body(): pl.pallas_call(functools.partial(kernel, times, groups, factor), out_shap...  93.6 us
    pallas_call x1, Pallas kernels, body(): pl.pallas_call(settle, out_shape=[jax.ShapeDtypeStruct(chunk, jnp.bfloat1...  1.98 us

profile of v4, /device:TPU:0, one launch (start us, length us, event | category | flops | bytes accessed | tf_op | source)
XLA Modules:
  0.0 96.3 jit_solution(15667536504551291246)
XLA Ops:
  0.6 93.6 %shard_map.59 = (bf16[2,512,256]{2,1,0:T(8,128)(2,1)}, bf16[2,512,256]{2,1,0:T(8,128)(2,1)}) custom-call(bf16[2,192,512]{2,1,0:T(8,128)(2,1)} %bitcast.11, bf16[2,192,2048]{2,1,0:T(8,128)(2,1)} %bitcast.10, s32[1,3]{1,0:T(1,128)} %momenta_ref.1, bf16[2,2048,256]{2,1,0:T(8,128)(2,1)} %bitcast.9), custom_call_target="tpu_custom_call" | custom-call | tf_op jit(solution)/shard_map/pallas_call | solution.py:503
  94.3 2.0 %shard_map.60 = (bf16[2,512,256]{2,1,0:T(8,128)(2,1)}, bf16[2,512,256]{2,1,0:T(8,128)(2,1)}) custom-call(bf16[2,512,256]{2,1,0:T(8,128)(2,1)} %get-tuple-element.6.meson_in, bf16[2,512,256]{2,1,0:T(8,128)(2,1)} %get-tuple-element.7.product_in), custom_call_target="tpu_custom_call" | custom-call | tf_op jit(solution)/shard_map/pallas_call | solution.py:560

commit v5 on v4

--- a/solution.py
+++ b/solution.py
@@ -177,12 +177,22 @@
         both = jnp.dot(phased[...], right, preferred_element_type=jnp.float32)
         return both.reshape(2, rows, cols)
 
-    def x_copy(dest):
-        return send(x_out.at[dest], x_in.at[dest], xo_sem.at[dest], xi_sem.at[dest], mate)
-
-    def z_copy(dest, side, site):
+    def x_copy(dest, part):
         return send(
-            z_out.at[dest], z_in.at[dest, side], zo_sem.at[dest], zi_sem.at[dest, side], site
+            x_out.at[dest, part],
+            x_in.at[dest, part],
+            xo_sem.at[dest, part],
+            xi_sem.at[dest, part],
+            mate,
+        )
+
+    def z_copy(dest, part, side, site):
+        return send(
+            z_out.at[dest, part],
+            z_in.at[dest, side, part],
+            zo_sem.at[dest, part],
+            zi_sem.at[dest, side, part],
+            site,
         )
 
     def t_copy(dest, side, site):
@@ -195,8 +205,9 @@
     def first(k, carry):
         dest = order(k, z, nz)
         theirs = partial(dest * PAIR + (1 - x))
-        x_out[dest] = theirs[:, thin:].astype(jnp.bfloat16)
-        x_copy(dest).start()
+        for part in range(2):
+            x_out[dest, part] = theirs[part, thin:].astype(jnp.bfloat16)
+            x_copy(dest, part).start()
         kept[dest, 1, :, :thin] = theirs[:, :thin]
         kept[dest, 0] = partial(dest * PAIR + x)
 
@@ -224,30 +235,71 @@
 
     lax.fori_loop(0, nz, first, 0)
 
+    def block(site):
+        return gathered.at[site]
+
+    def slim(ref):
+        return ref.at[:, pl.ds(0, thin), :]
+
+    def rest(site, part):
+        return gathered.at[site, part, pl.ds(thin, rows - thin), :]
+
+    def pair(site):
+        first_of = pl.multiple_of(site // PAIR * PAIR, PAIR)
+        return gathered.at[pl.ds(first_of, PAIR), :, pl.ds(0, thin), :]
+
+    def rest_copy(site, part, sem, to):
+        src = rest(site, part)
+        return send(src, src, sem.at[site // PAIR, part], g_recv.at[site, part], to)
+
+    def to_up(site, part):
+        return rest_copy(site, part, g_up, up)
+
+    def to_down(site, part):
+        return rest_copy(site, part, g_down, down)
+
+    def to_mate(site, part):
+        return rest_copy(site, part, g_pair, mate)
+
     def second(k, carry):
         dest = order(k, z, nz)
-        x_copy(dest).wait_recv()
-        kept[dest, 0, :, thin:] += x_in[dest].astype(jnp.float32)
-
-        @pl.when((dest >= z) & has_down)
-        def _():
-            z_copy(dest, 0, up).wait_recv()
-            kept[dest, 0, :, thin:] += z_in[dest, 0].astype(jnp.float32)
-
-        @pl.when((dest <= z) & has_up)
-        def _():
-            z_copy(dest, 1, down).wait_recv()
-            kept[dest, 0, :, thin:] += z_in[dest, 1].astype(jnp.float32)
-
-        @pl.when(dest > z)
-        def _():
-            z_out[dest] = kept[dest, 0, :, thin:].astype(jnp.bfloat16)
-            z_copy(dest, 0, up).start()
-
-        @pl.when(dest < z)
-        def _():
-            z_out[dest] = kept[dest, 0, :, thin:].astype(jnp.bfloat16)
-            z_copy(dest, 1, down).start()
+        for part in range(2):
+            x_copy(dest, part).wait_recv()
+            kept[dest, 0, part, thin:] += x_in[dest, part].astype(jnp.float32)
+
+            @pl.when((dest >= z) & has_down)
+            def _():
+                z_copy(dest, part, 0, up).wait_recv()
+                kept[dest, 0, part, thin:] += z_in[dest, 0, part].astype(jnp.float32)
+
+            @pl.when((dest <= z) & has_up)
+            def _():
+                z_copy(dest, part, 1, down).wait_recv()
+                kept[dest, 0, part, thin:] += z_in[dest, 1, part].astype(jnp.float32)
+
+            @pl.when(dest > z)
+            def _():
+                z_out[dest, part] = kept[dest, 0, part, thin:].astype(jnp.bfloat16)
+                z_copy(dest, part, 0, up).start()
+
+            @pl.when(dest < z)
+            def _():
+                z_out[dest, part] = kept[dest, 0, part, thin:].astype(jnp.bfloat16)
+                z_copy(dest, part, 1, down).start()
+
+            @pl.when(dest == z)
+            def _():
+                gathered[me, part, thin:] = kept[z, 0, part, thin:].astype(jnp.bfloat16)
+
+                @pl.when(has_up)
+                def _():
+                    to_up(me, part).start()
+
+                @pl.when(has_down)
+                def _():
+                    to_down(me, part).start()
+
+                to_mate(me, part).start()
 
         @pl.when(k == 0)
         def _():
@@ -269,29 +321,7 @@
     lax.fori_loop(0, nz, second, 0)
     m_copy.wait_recv()
     kept[z, 0, :, :thin] += m_in[...].astype(jnp.float32)
-    gathered[me] = kept[z, 0].astype(jnp.bfloat16)
-
-    def block(site):
-        return gathered.at[site]
-
-    def slim(ref):
-        return ref.at[:, pl.ds(0, thin), :]
-
-    def rest(site):
-        return gathered.at[site, :, pl.ds(thin, rows - thin), :]
-
-    def pair(site):
-        first_of = pl.multiple_of(site // PAIR * PAIR, PAIR)
-        return gathered.at[pl.ds(first_of, PAIR), :, pl.ds(0, thin), :]
-
-    def to_up(site):
-        return send(rest(site), rest(site), g_up.at[site // PAIR], g_recv.at[site], up)
-
-    def to_down(site):
-        return send(rest(site), rest(site), g_down.at[site // PAIR], g_recv.at[site], down)
-
-    def to_mate(site):
-        return send(rest(site), rest(site), g_pair.at[site // PAIR], g_recv.at[site], mate)
+    gathered[me, :, :thin] = kept[z, 0, :, :thin].astype(jnp.bfloat16)
 
     def slim_up(site):
         line = site // PAIR
@@ -305,17 +335,7 @@
         return send(slim(block(site)), slim(block(site)), s_pair, s_recv.at[z], mate)
 
     own = block(me)
-
-    @pl.when(has_up)
-    def _():
-        to_up(me).start()
-
-    @pl.when(has_down)
-    def _():
-        to_down(me).start()
-
     slim_mate(me).start()
-    to_mate(me).start()
     meson_copy = pltpu.make_async_copy(own, meson_ref, leave.at[0])
     meson_copy.start()
 
@@ -354,29 +374,31 @@
         below = me - d * PAIR
         above = me + d * PAIR
 
-        @pl.when(z >= d)
-        def _():
-            to_up(below).wait_recv()
-
-            @pl.when(has_up)
-            def _():
-                to_up(below).start()
-
-            to_mate(below).start()
+        for part in range(2):
+
+            @pl.when(z >= d)
+            def _():
+                to_up(below, part).wait_recv()
+
+                @pl.when(has_up)
+                def _():
+                    to_up(below, part).start()
+
+                to_mate(below, part).start()
+
+            @pl.when(z + d < nz)
+            def _():
+                to_down(above, part).wait_recv()
+
+                @pl.when(has_down)
+                def _():
+                    to_down(above, part).start()
+
+                to_mate(above, part).start()
 
         @pl.when((z == d) & has_up)
         def _():
             slim_up(me).start()
-
-        @pl.when(z + d < nz)
-        def _():
-            to_down(above).wait_recv()
-
-            @pl.when(has_down)
-            def _():
-                to_down(above).start()
-
-            to_mate(above).start()
 
         @pl.when((z + d == nz - 1) & has_down)
         def _():
@@ -422,13 +444,15 @@
         @pl.when(z >= d)
         def _():
             site = mate - d * PAIR
-            to_mate(site).wait_recv()
+            to_mate(site, 0).wait_recv()
+            to_mate(site, 1).wait_recv()
             arrive(site)
 
         @pl.when((z + d < nz) & (d > 0))
         def _():
             site = mate + d * PAIR
-            to_mate(site).wait_recv()
+            to_mate(site, 0).wait_recv()
+            to_mate(site, 1).wait_recv()
             arrive(site)
 
         return carry
@@ -442,23 +466,32 @@
         copies.append(copy)
 
     def drain(k, carry):
-        x_copy(k).wait_send()
+        for part in range(2):
+            x_copy(k, part).wait_send()
+            to_mate(k * PAIR + x, part).wait_send()
+
+            @pl.when(k != z)
+            def _():
+                z_copy(k, part, 0, mate).wait_send()
+
+            @pl.when((k <= z) & has_up)
+            def _():
+                to_up(k * PAIR + x, part).wait_send()
+
+            @pl.when((k >= z) & has_down)
+            def _():
+                to_down(k * PAIR + x, part).wait_send()
 
         @pl.when(k != z)
         def _():
-            z_copy(k, 0, mate).wait_send()
             t_copy(k, 0, mate).wait_send()
 
-        to_mate(k * PAIR + x).wait_send()
-
         @pl.when((k <= z) & has_up)
         def _():
-            to_up(k * PAIR + x).wait_send()
             slim_up(k * PAIR).wait_send()
 
         @pl.when((k >= z) & has_down)
         def _():
-            to_down(k * PAIR + x).wait_send()
             slim_down(k * PAIR).wait_send()
 
         return carry
@@ -521,14 +554,14 @@
             pltpu.VMEM(chunk, jnp.float32),
             dma(()),
             dma(()),
-            dma((nz,)),
-            dma((nz,)),
-            dma((nz,)),
             dma((nz, 2)),
-            dma((groups,)),
-            dma((nz,)),
-            dma((nz,)),
-            dma((nz,)),
+            dma((nz, 2)),
+            dma((nz, 2)),
+            dma((nz, 2, 2)),
+            dma((groups, 2)),
+            dma((nz, 2)),
+            dma((nz, 2)),
+            dma((nz, 2)),
             dma((nz,)),
             dma((nz,)),
             dma((nz,)),

time: 96.4 us -> 96.5 us (level)
  no operation moved by 1% of the time
where the time goes in v5:
time: 96.5 us; the launch traced here: 96.3 us
  Pallas kernels  95.7 us (99%)
    pallas_call x1, Pallas kernels, body(): pl.pallas_call(functools.partial(kernel, times, groups, factor), out_shap...  93.7 us
    pallas_call x1, Pallas kernels, body(): pl.pallas_call(settle, out_shape=[jax.ShapeDtypeStruct(chunk, jnp.bfloat1...  1.98 us

profile of v5, /device:TPU:0, one launch (start us, length us, event | category | flops | bytes accessed | tf_op | source)
XLA Modules:
  0.0 96.3 jit_solution(12265095253148180536)
XLA Ops:
  0.6 93.7 %shard_map.59 = (bf16[2,512,256]{2,1,0:T(8,128)(2,1)}, bf16[2,512,256]{2,1,0:T(8,128)(2,1)}) custom-call(bf16[2,192,512]{2,1,0:T(8,128)(2,1)} %bitcast.11, bf16[2,192,2048]{2,1,0:T(8,128)(2,1)} %bitcast.10, s32[1,3]{1,0:T(1,128)} %momenta_ref.1, bf16[2,2048,256]{2,1,0:T(8,128)(2,1)} %bitcast.9), custom_call_target="tpu_custom_call" | custom-call | tf_op jit(solution)/shard_map/pallas_call | solution.py:536
  94.3 2.0 %shard_map.60 = (bf16[2,512,256]{2,1,0:T(8,128)(2,1)}, bf16[2,512,256]{2,1,0:T(8,128)(2,1)}) custom-call(bf16[2,512,256]{2,1,0:T(8,128)(2,1)} %get-tuple-element.6.meson_in, bf16[2,512,256]{2,1,0:T(8,128)(2,1)} %get-tuple-element.7.product_in), custom_call_target="tpu_custom_call" | custom-call | tf_op jit(solution)/shard_map/pallas_call | solution.py:593

commit v6 on v5

--- a/solution.py
+++ b/solution.py
@@ -26,7 +26,7 @@
 
 
 def thin_rows(rows):
-    return max(16, rows // 6 // 16 * 16)
+    return max(16, rows * 3 // 16 // 16 * 16)
 
 
 def order(k, z, nz):

time: 96.5 us -> 96.8 us (level)
  no operation moved by 1% of the time
where the time goes in v6:
time: 96.8 us; the launch traced here: 96.7 us
  Pallas kernels  96 us (99%)
    pallas_call x1, Pallas kernels, body(): pl.pallas_call(functools.partial(kernel, times, groups, factor), out_shap...  94 us
    pallas_call x1, Pallas kernels, body(): pl.pallas_call(settle, out_shape=[jax.ShapeDtypeStruct(chunk, jnp.bfloat1...  1.98 us

profile of v6, /device:TPU:0, one launch (start us, length us, event | category | flops | bytes accessed | tf_op | source)
XLA Modules:
  0.0 96.7 jit_solution(8102853049564700670)
XLA Ops:
  0.6 94.0 %shard_map.59 = (bf16[2,512,256]{2,1,0:T(8,128)(2,1)}, bf16[2,512,256]{2,1,0:T(8,128)(2,1)}) custom-call(bf16[2,192,512]{2,1,0:T(8,128)(2,1)} %bitcast.11, bf16[2,192,2048]{2,1,0:T(8,128)(2,1)} %bitcast.10, s32[1,3]{1,0:T(1,128)} %momenta_ref.1, bf16[2,2048,256]{2,1,0:T(8,128)(2,1)} %bitcast.9), custom_call_target="tpu_custom_call" | custom-call | tf_op jit(solution)/shard_map/pallas_call | solution.py:536
  94.7 2.0 %shard_map.60 = (bf16[2,512,256]{2,1,0:T(8,128)(2,1)}, bf16[2,512,256]{2,1,0:T(8,128)(2,1)}) custom-call(bf16[2,512,256]{2,1,0:T(8,128)(2,1)} %get-tuple-element.6.meson_in, bf16[2,512,256]{2,1,0:T(8,128)(2,1)} %get-tuple-element.7.product_in), custom_call_target="tpu_custom_call" | custom-call | tf_op jit(solution)/shard_map/pallas_call | solution.py:593

commit v7 on v6

--- a/solution.py
+++ b/solution.py
@@ -26,7 +26,7 @@
 
 
 def thin_rows(rows):
-    return max(16, rows * 3 // 16 // 16 * 16)
+    return max(16, rows // 8 // 16 * 16)
 
 
 def order(k, z, nz):

time: 96.8 us -> 96.1 us (level)
  no operation moved by 1% of the time
where the time goes in v7:
time: 96.1 us; the launch traced here: 96 us
  Pallas kernels  95.3 us (99%)
    pallas_call x1, Pallas kernels, body(): pl.pallas_call(functools.partial(kernel, times, groups, factor), out_shap...  93.3 us
    pallas_call x1, Pallas kernels, body(): pl.pallas_call(settle, out_shape=[jax.ShapeDtypeStruct(chunk, jnp.bfloat1...  1.98 us

profile of v7, /device:TPU:0, one launch (start us, length us, event | category | flops | bytes accessed | tf_op | source)
XLA Modules:
  0.0 96.0 jit_solution(9498145559791750449)
XLA Ops:
  0.6 93.3 %shard_map.59 = (bf16[2,512,256]{2,1,0:T(8,128)(2,1)}, bf16[2,512,256]{2,1,0:T(8,128)(2,1)}) custom-call(bf16[2,192,512]{2,1,0:T(8,128)(2,1)} %bitcast.11, bf16[2,192,2048]{2,1,0:T(8,128)(2,1)} %bitcast.10, s32[1,3]{1,0:T(1,128)} %momenta_ref.1, bf16[2,2048,256]{2,1,0:T(8,128)(2,1)} %bitcast.9), custom_call_target="tpu_custom_call" | custom-call | tf_op jit(solution)/shard_map/pallas_call | solution.py:536
  94.0 2.0 %shard_map.60 = (bf16[2,512,256]{2,1,0:T(8,128)(2,1)}, bf16[2,512,256]{2,1,0:T(8,128)(2,1)}) custom-call(bf16[2,512,256]{2,1,0:T(8,128)(2,1)} %get-tuple-element.6.meson_in, bf16[2,512,256]{2,1,0:T(8,128)(2,1)} %get-tuple-element.7.product_in), custom_call_target="tpu_custom_call" | custom-call | tf_op jit(solution)/shard_map/pallas_call | solution.py:593
